TPU v7x, 32 devices: a whole 2x2x4 slice. The times are simulated.
32 devices in a mesh: ep: 16 (over z, y, x), tp: 2 (over core).
Axes of the slice: x: 2, y: 2, z: 4, core: 2. Of those that a mesh axis runs over, the one named last changes fastest.
Arguments:
- tokens: bfloat16 [4096, 4096], P(('ep', 'tp')), may hold values from -6 to 6
- expert_ids: int32 [4096, 8], P(('ep', 'tp')), may hold values from 0 to 127, as said below
- gate_weights: float32 [4096, 8], P(('ep', 'tp')), may hold values from 0.1 to 1
- grad_out: bfloat16 [4096, 4096], P(('ep', 'tp')), may hold values from -6 to 6
- w_gate: bfloat16 [16, 768, 4096], P('ep', 'tp'), may hold values from -0.09375 to 0.09375
- w_up: bfloat16 [16, 768, 4096], P('ep', 'tp'), may hold values from -0.09375 to 0.09375
- w_down: bfloat16 [16, 768, 4096], P('ep', 'tp'), may hold values from -0.21875 to 0.21875
Outputs:
- grad_tokens: bfloat16 [4096, 4096], P(('ep', 'tp'))
- grad_gate: bfloat16 [16, 768, 4096], P('ep', 'tp')
- grad_up: bfloat16 [16, 768, 4096], P('ep', 'tp')
- grad_down: bfloat16 [16, 768, 4096], P('ep', 'tp')
Inputs may be any that keep to these rules, and one draw needn't show every extreme that they name: `expert_ids`: each token names 8 different experts. No expert below 16 is named by more than 8 tokens of one device's rows, and in every draw some expert below 16 is named by exactly 8 tokens of every device's rows.
All inputs are finite; a program needn't handle non-finite values.
Results may differ from a plain program's by a relative error of at most 0.0064.
Values may be sent and summed in bfloat16 or wider, within the bound.
No kernel may reach another device: no remote copies, remote signals or barrier semaphores. Data moves between devices by JAX's collectives and lax.ppermute only.
A program may use at most 192 MiB of HBM per device.

v0:
```python
import functools

import jax
import jax.numpy as jnp
from jax import lax
from jax.experimental import pallas as pl
from jax.experimental.pallas import tpu as pltpu
from jax.sharding import PartitionSpec as P


CAP = 8
MIB = 1 << 20
PIECES = 2
IN_FLIGHT = 3

f32 = jnp.float32
bf16 = jnp.bfloat16


def in_hbm(x):
    return pltpu.with_memory_space_constraint(x, pltpu.HBM)


def in_vmem(x):
    return pltpu.with_memory_space_constraint(x, pltpu.VMEM)


def route(experts, ids_ref, gates_ref, match_ref, gate_s):
    rows, count = match_ref.shape
    expert_at = lax.broadcasted_iota(jnp.int32, (experts, count), 0)
    member = jnp.zeros((experts, count), f32)
    for k in range(ids_ref.shape[0]):
        member += jnp.where(ids_ref[k : k + 1, :] == expert_at, 1.0, 0.0)
    earlier = jnp.where(
        lax.broadcasted_iota(jnp.int32, (count, count), 0)
        < lax.broadcasted_iota(jnp.int32, (count, count), 1),
        1.0,
        0.0,
    ).astype(bf16)
    before = jnp.dot(member.astype(bf16), earlier, preferred_element_type=f32)
    row = lax.broadcasted_iota(jnp.int32, (rows, count), 0)
    match = jnp.zeros((rows, count), f32)
    gate = jnp.zeros((rows, count), f32)
    for k in range(ids_ref.shape[0]):
        named = ids_ref[k : k + 1, :]
        place = jnp.sum(
            jnp.where(named == expert_at, before, 0.0), axis=0, keepdims=True
        ).astype(jnp.int32)
        hit = jnp.where(named < experts, named * CAP + place, -1) == row
        match = jnp.where(hit, 1.0, match)
        gate = jnp.where(hit, gates_ref[k : k + 1, :], gate)
    match_ref[...] = match.astype(bf16)
    gate_s[...] = jnp.broadcast_to(jnp.sum(gate, axis=1, keepdims=True), gate_s.shape)


def gather_kernel(
    experts, ids_ref, gates_ref, tok_ref, dy_ref, send_ref, match_ref,
    ids_s, gates_s, rows_s, match_s, gate_s, out_s, sems, out_sems,
):
    blocks, _, block = rows_s.shape
    half = blocks // 2
    small = [
        pltpu.make_async_copy(ids_ref, ids_s, sems.at[blocks]),
        pltpu.make_async_copy(gates_ref, gates_s, sems.at[blocks + 1]),
    ]

    def load(i):
        src = tok_ref if i < half else dy_ref
        cols = pl.ds(i % half * block, block)
        return pltpu.make_async_copy(src.at[:, cols], rows_s.at[i], sems.at[i])

    def store(i):
        cols = pl.ds(i * block, block)
        return pltpu.make_async_copy(out_s.at[i], send_ref.at[:, cols], out_sems.at[i])

    for copy in small:
        copy.start()
    for i in range(blocks):
        load(i).start()
    for copy in small:
        copy.wait()
    route(experts, ids_s, gates_s, match_s, gate_s)
    keep = pltpu.make_async_copy(match_s, match_ref, out_sems.at[blocks])
    for i in range(blocks):
        load(i).wait()
        picked = jnp.dot(match_s[...], rows_s[i], preferred_element_type=f32)
        if i >= half:
            picked = gate_s[:, :1] * picked
        out_s[i] = picked.astype(bf16)
        store(i).start()
    keep.start()
    for i in range(blocks):
        store(i).wait()
    keep.wait()


def gather(experts, ids, gates, tokens, grad_out):
    count, width = tokens.shape
    rows = experts * CAP
    blocks = 8
    block = 2 * width // blocks
    anywhere = pl.BlockSpec(memory_space=pl.ANY)
    return pl.pallas_call(
        functools.partial(gather_kernel, experts),
        in_specs=[anywhere] * 4,
        out_specs=[anywhere] * 2,
        out_shape=[pltpu.HBM((rows, 2 * width), bf16), pltpu.HBM((rows, count), bf16)],
        scratch_shapes=[
            pltpu.VMEM(ids.shape, ids.dtype),
            pltpu.VMEM(gates.shape, gates.dtype),
            pltpu.VMEM((blocks, count, block), bf16),
            pltpu.VMEM((rows, count), bf16),
            pltpu.VMEM((rows, 128), f32),
            pltpu.VMEM((blocks, rows, block), bf16),
            pltpu.SemaphoreType.DMA((blocks + 2,)),
            pltpu.SemaphoreType.DMA((blocks + 1,)),
        ],
        name="gather",
        cost_estimate=pl.CostEstimate(
            flops=4 * rows * count * width, bytes_accessed=4 * width * (rows + count), transcendentals=0
        ),
        compiler_params=pltpu.CompilerParams(
            vmem_limit_bytes=8 * MIB + 8 * width * (rows + count)
        ),
    )(in_hbm(ids), in_hbm(gates), in_hbm(tokens), in_hbm(grad_out))


def expert_kernel(
    recv_ref, gate_a, up_a, down_a, gate_b, up_b, down_b, ret_ref, own_ref, partner_ref,
    turned_s, joined_s, down_s, first_s, fold_s, total_s, coef_s, out_s, sems, coef_sems, out_sems,
):
    hidden = gate_a.shape[0]
    blocks, _, block = out_s.shape
    width = blocks * block

    size = hidden // PIECES
    units = [(h, k, p * size, size) for h in range(2) for k in range(3) for p in range(PIECES)]
    sources = ((gate_a, up_a, down_a), (gate_b, up_b, down_b))

    def held(h, k, at, size):
        if k == 2:
            return down_s.at[h, pl.ds(at, size)]
        return joined_s.at[h, pl.ds(k * hidden + at, size)]

    def load(n):
        h, k, at, size = units[n]
        return pltpu.make_async_copy(
            sources[h][k].at[pl.ds(at, size)], held(h, k, at, size), sems.at[n]
        )

    def store(i):
        return pltpu.make_async_copy(
            out_s.at[i], ret_ref.at[:, pl.ds(i * block, block)], out_sems.at[i]
        )

    for n in range(IN_FLIGHT):
        load(n).start()

    for side in range(2):
        for i in range(blocks):
            at = i * block
            turned_s[side, at : at + block, :] = recv_ref[
                :, side * width + at : side * width + at + block
            ].T
    kept = []
    for h, coef_ref in enumerate((own_ref, partner_ref)):
        for n, (half, k, at, size) in enumerate(units):
            if half != h:
                continue
            load(n).wait()
            if n + IN_FLIGHT < len(units):
                load(n + IN_FLIGHT).start()
            first_s[k * hidden + at : k * hidden + at + size, :] = jnp.dot(
                held(h, k, at, size)[...], turned_s[k // 2], preferred_element_type=f32
            )

        step = 32

        @pl.loop(0, hidden // step)
        def _(b):
            at = pl.multiple_of(b * step, step)
            g = first_s[pl.ds(at, step), :]
            u = first_s[pl.ds(hidden + at, step), :]
            a = first_s[pl.ds(2 * hidden + at, step), :]
            s = jax.nn.sigmoid(g)
            d_pre = (a * u * s * (1.0 + g * (1.0 - s))).astype(bf16)
            d_up = (a * g * s).astype(bf16)
            coef_s[h, pl.ds(at, step), :] = d_pre
            coef_s[h, pl.ds(hidden + at, step), :] = d_up
            coef_s[h, pl.ds(2 * hidden + at, step), :] = (g * s * u).astype(bf16)

        kept.append(pltpu.make_async_copy(coef_s.at[h], coef_ref, coef_sems.at[h]))
        fold_s[...] = coef_s[h, : 2 * hidden, :].T
        for i in range(blocks):
            part = jnp.dot(
                fold_s[...],
                joined_s[h, :, i * block : (i + 1) * block],
                preferred_element_type=f32,
            )
            if h == 0:
                total_s[i] = part
            else:
                out_s[i] = (total_s[i] + part).astype(bf16)
                store(i).start()
        kept[h].start()
    for i in range(blocks):
        store(i).wait()
    for copy in kept:
        copy.wait()


def expert_terms(recv, own, partner):
    rows, width = recv.shape[0], recv.shape[1] // 2
    hidden = own[0].shape[0]
    blocks = 4
    block = width // blocks
    anywhere = pl.BlockSpec(memory_space=pl.ANY)
    vmem = pl.BlockSpec(memory_space=pltpu.VMEM)
    coef = pltpu.HBM((3 * hidden, rows), bf16)
    return pl.pallas_call(
        expert_kernel,
        in_specs=[vmem] + [anywhere] * 6,
        out_specs=[anywhere] * 3,
        out_shape=[pltpu.HBM((rows, width), bf16), coef, coef],
        scratch_shapes=[
            pltpu.VMEM((2, width, rows), bf16),
            pltpu.VMEM((2, 2 * hidden, width), bf16),
            pltpu.VMEM((2, hidden, width), bf16),
            pltpu.VMEM((3 * hidden, rows), f32),
            pltpu.VMEM((rows, 2 * hidden), bf16),
            pltpu.VMEM((blocks, rows, block), f32),
            pltpu.VMEM((2, 3 * hidden, rows), bf16),
            pltpu.VMEM((blocks, rows, block), bf16),
            pltpu.SemaphoreType.DMA((6 * PIECES,)),
            pltpu.SemaphoreType.DMA((2,)),
            pltpu.SemaphoreType.DMA((blocks,)),
        ],
        name="expert_terms",
        cost_estimate=pl.CostEstimate(
            flops=20 * rows * hidden * width,
            bytes_accessed=12 * hidden * width + 6 * rows * width,
            transcendentals=2 * rows * hidden,
        ),
        compiler_params=pltpu.CompilerParams(
            vmem_limit_bytes=min(
                8 * MIB + 12 * hidden * width + 18 * rows * width, 65408 * 1024 - 4 * rows * width
            )
        ),
    )(in_vmem(recv), *(in_hbm(w) for w in (*own, *partner)))


def weight_kernel(coef_a, coef_b, x_a, dy_a, x_b, dy_b, gate_ref, up_ref, down_ref):
    hidden = gate_ref.shape[0]
    x = jnp.concatenate([x_a[...], x_b[...]], axis=0)
    dy = jnp.concatenate([dy_a[...], dy_b[...]], axis=0)
    for k, (out, right) in enumerate(((gate_ref, x), (up_ref, x), (down_ref, dy))):
        at = slice(k * hidden, (k + 1) * hidden)
        left = jnp.concatenate([coef_a[at, :], coef_b[at, :]], axis=1)
        out[...] = jnp.dot(left, right, preferred_element_type=f32).astype(bf16)


def weight_grads(coef_a, coef_b, rows_a, rows_b):
    rows, width = rows_a.shape[0], rows_a.shape[1] // 2
    hidden = coef_a.shape[0] // 3
    block = 512
    blocks = width // block
    whole = lambda i: (0, 0)
    x_at = pl.BlockSpec((rows, block), lambda i: (0, i))
    dy_at = pl.BlockSpec((rows, block), lambda i: (0, blocks + i))
    rows_a, rows_b = in_hbm(rows_a), in_hbm(rows_b)
    return pl.pallas_call(
        weight_kernel,
        grid=(blocks,),
        in_specs=[pl.BlockSpec(coef_a.shape, whole)] * 2 + [x_at, dy_at] * 2,
        out_specs=[pl.BlockSpec((hidden, block), lambda i: (0, i))] * 3,
        out_shape=[jax.ShapeDtypeStruct((hidden, width), bf16)] * 3,
        name="weight_grads",
        cost_estimate=pl.CostEstimate(
            flops=12 * rows * hidden * width,
            bytes_accessed=6 * hidden * width + 8 * rows * width,
            transcendentals=0,
        ),
        compiler_params=pltpu.CompilerParams(vmem_limit_bytes=65472 * 1024),
    )(in_hbm(coef_a), in_hbm(coef_b), rows_a, rows_a, rows_b, rows_b)


def combine_kernel(turned_ref, ret_ref, out_ref, turned_s, ret_s, out_s, sems, out_sems):
    blocks, _, block = ret_s.shape

    def load(i):
        cols = pl.ds(i * block, block)
        return pltpu.make_async_copy(ret_ref.at[:, cols], ret_s.at[i], sems.at[i])

    def store(i):
        cols = pl.ds(i * block, block)
        return pltpu.make_async_copy(out_s.at[i], out_ref.at[:, cols], out_sems.at[i])

    first = pltpu.make_async_copy(turned_ref, turned_s, sems.at[blocks])
    first.start()
    for i in range(blocks):
        load(i).start()
    first.wait()
    for i in range(blocks):
        load(i).wait()
        out_s[i] = jnp.dot(turned_s[...], ret_s[i], preferred_element_type=f32).astype(bf16)
        store(i).start()
    for i in range(blocks):
        store(i).wait()


def combine(turned, ret):
    count, rows = turned.shape
    width = ret.shape[1]
    blocks = 4
    block = width // blocks
    anywhere = pl.BlockSpec(memory_space=pl.ANY)
    return pl.pallas_call(
        combine_kernel,
        in_specs=[anywhere] * 2,
        out_specs=anywhere,
        out_shape=pltpu.HBM((count, width), bf16),
        scratch_shapes=[
            pltpu.VMEM((count, rows), bf16),
            pltpu.VMEM((blocks, rows, block), bf16),
            pltpu.VMEM((blocks, count, block), bf16),
            pltpu.SemaphoreType.DMA((blocks + 1,)),
            pltpu.SemaphoreType.DMA((blocks,)),
        ],
        name="combine",
        cost_estimate=pl.CostEstimate(
            flops=2 * rows * count * width, bytes_accessed=2 * (rows + count) * width, transcendentals=0
        ),
        compiler_params=pltpu.CompilerParams(
            vmem_limit_bytes=8 * MIB + 4 * (rows + count) * width
        ),
    )(in_hbm(turned), in_hbm(ret))


def exchange(rows):
    return lax.all_to_all(rows, "ep", split_axis=0, concat_axis=0, tiled=True)


def swap(value):
    return lax.ppermute(value, "tp", [(0, 1), (1, 0)])


def local(tokens, expert_ids, gate_weights, grad_out, w_gate, w_up, w_down):
    experts = lax.axis_size("ep")
    own = (w_gate[0], w_up[0], w_down[0])
    send, match = gather(experts, expert_ids.T, gate_weights.T, tokens, grad_out)
    recv = exchange(send)
    partner = tuple(swap(w) for w in own)
    turned = match.T
    ret, coef, coef_sent = expert_terms(recv, own, partner)
    back = exchange(ret)
    coef_got, rows_got = swap(coef_sent), swap(recv)
    grads = weight_grads(coef, coef_got, recv, rows_got)
    grad_tokens = combine(turned, back)
    return (grad_tokens, *(g[None] for g in grads))


def solution(mesh):
    rows = P(("ep", "tp"), None)
    weight = P("ep", "tp", None)
    return jax.shard_map(
        local,
        mesh=mesh,
        in_specs=(rows, rows, rows, rows, weight, weight, weight),
        out_specs=(rows, weight, weight, weight),
        check_vma=False,
    )
```

profile of v0, /device:TPU:8, one launch (start us, length us, event | category | flops | bytes accessed | tf_op | source)
XLA Modules:
  0.0 116.2 jit_solution(8365842869134498299)
XLA Ops:
  0.6 3.6 %gather.1 = (bf16[128,8192]{1,0:T(8,128)(2,1)}, bf16[128,128]{1,0:T(8,128)(2,1)}) custom-call(s32[8,128]{1,0:T(8,128)} %bitcast.27, f32[8,128]{1,0:T(8,128)} %bitcast.28, bf16[128,4096]{1,0:T(8,128)(2,1)} %tok_ref.1, bf16[128,4096]{1,0:T(8,128)(2,1)} %dy_ref.1), custom_call_target="tpu_custom_call" | custom-call | flops 268435456 | bytes 4194304 | tf_op jit(solution)/shard_map/gather/pallas_call | solution.py:103
  4.3 7.2 %all-to-all-start = ((bf16[16,8,8192]{2,1,0:T(8,128)(2,1)}), bf16[16,8,8192]{2,1,0:T(8,128)(2,1)S(1)}, u32[]{:S(2)}, u32[]{:S(2)}) async-start(bf16[16,8,8192]{2,1,0:T(8,128)(2,1)} %bitcast.24), calls=%async_computation | async-start | bytes 4194304 | tf_op jit(solution)/shard_map/all_to_all | solution.py:340
  11.5 0.0 collective-permute-start
  11.5 0.5 collective-permute-start.1
  12.0 0.1 collective-permute-start.2
  12.1 46.6 %all-to-all-done = bf16[16,8,8192]{2,1,0:T(8,128)(2,1)S(1)} async-done(((bf16[16,8,8192]{2,1,0:T(8,128)(2,1)}), bf16[16,8,8192]{2,1,0:T(8,128)(2,1)S(1)}, u32[]{:S(2)}, u32[]{:S(2)}) %all-to-all-start) | async-done | bytes 2097184 | tf_op jit(solution)/shard_map/all_to_all | solution.py:340
  58.7 0.0 copy-start
  58.7 0.0 copy-start.3
  58.7 0.0 collective-permute-start.4
  58.7 0.0 collective-permute-done.gate_b
  58.7 0.0 collective-permute-done.1.up_b
  58.7 0.0 collective-permute-done.2.down_b
  58.8 12.2 %expert_terms.1 = (bf16[128,4096]{1,0:T(8,128)(2,1)}, bf16[1152,128]{1,0:T(8,128)(2,1)}, bf16[1152,128]{1,0:T(8,128)(2,1)}) custom-call(bf16[128,8192]{1,0:T(8,128)(2,1)S(1)} %bitcast.14, bf16[384,4096]{1,0:T(8,128)(2,1)} %bitcast.19, bf16[384,4096]{1,0:T(8,128)(2,1)} %bitcast.21, bf16[384,4096]{1,0:T(8,128)(2,1)} %bitcast.23, ...), custom_call_target="tpu_custom_call" | custom-call | flops 4026531840 | bytes 22020096 | tf_op jit(solution)/shard_map/expert_terms/pallas_call | solution.py:220
  71.0 0.0 copy-done
  71.0 5.8 %all-to-all-start.1 = ((bf16[16,8,4096]{2,1,0:T(8,128)(2,1)}), bf16[16,8,4096]{2,1,0:T(8,128)(2,1)S(1)}, u32[]{:S(2)}, u32[]{:S(2)}) async-start(bf16[16,8,4096]{2,1,0:T(8,128)(2,1)} %bitcast.25), calls=%async_computation.1 | async-start | bytes 2097152 | tf_op jit(solution)/shard_map/all_to_all | solution.py:340
  76.8 0.0 collective-permute-start.3
  76.8 0.0 copy-done.3
  76.8 0.7 copy.11
  77.6 24.7 %all-to-all-done.1 = bf16[16,8,4096]{2,1,0:T(8,128)(2,1)S(1)} async-done(((bf16[16,8,4096]{2,1,0:T(8,128)(2,1)}), bf16[16,8,4096]{2,1,0:T(8,128)(2,1)S(1)}, u32[]{:S(2)}, u32[]{:S(2)}) %all-to-all-start.1) | async-done | bytes 1048608 | tf_op jit(solution)/shard_map/all_to_all | solution.py:340
  102.3 0.0 copy-start.1
  102.3 1.0 copy-done.1
  103.2 2.6 %combine.1 = bf16[128,4096]{1,0:T(8,128)(2,1)} custom-call(bf16[128,128]{1,0:T(8,128)(2,1)} %bitcast.26, bf16[128,4096]{1,0:T(8,128)(2,1)} %bitcast.17), custom_call_target="tpu_custom_call" | custom-call | flops 134217728 | bytes 2097152 | tf_op jit(solution)/shard_map/combine/pallas_call | solution.py:317
  105.9 0.0 collective-permute-done.3.coef_b
  105.9 0.0 copy-start.2
  105.9 0.0 collective-permute-done.4.x_b.dy_b
  105.9 0.7 copy-done.2
  106.6 9.6 %weight_grads.1 = (bf16[384,4096]{1,0:T(8,128)(2,1)}, bf16[384,4096]{1,0:T(8,128)(2,1)}, bf16[384,4096]{1,0:T(8,128)(2,1)}) custom-call(bf16[1152,128]{1,0:T(8,128)(2,1)} %get-tuple-element.15.coef_a, bf16[1152,128]{1,0:T(8,128)(2,1)} %copy-done.2, bf16[128,8192]{1,0:T(8,128)(2,1)} %bitcast.15, bf16[128,8192]{1,0:T(8,128)(2,1)} %bitcast.16, ...), custom_call_target="tpu_custom_call" | custom-call | flops 2415919104 | bytes 13631488 | tf_op jit(solution)/shard_map/weight_grads/pallas_call | solution.py:271
Async XLA Ops:
  4.3 54.5 %all-to-all-start = ((bf16[16,8,8192]{2,1,0:T(8,128)(2,1)}), bf16[16,8,8192]{2,1,0:T(8,128)(2,1)S(1)}, u32[]{:S(2)}, u32[]{:S(2)}) async-start(bf16[16,8,8192]{2,1,0:T(8,128)(2,1)} %bitcast.24), calls=%async_computation | async-start | bytes 4194304 | tf_op jit(solution)/shard_map/all_to_all | solution.py:340
  11.5 47.2 %collective-permute-start = (bf16[384,4096]{1,0:T(8,128)(2,1)}, bf16[384,4096]{1,0:T(8,128)(2,1)}, u32[]{:S(2)}, u32[]{:S(2)}) collective-permute-start(bf16[384,4096]{1,0:T(8,128)(2,1)} %bitcast.18), channel_id=1, source_target_pairs={{0,1},{1,0},{2,3},{3,2},{4,5},{5,4},{6,7},{7,6},{8,9},{9,8},{10,11... | collective-permute-start | bytes 9437192 | tf_op jit(solution)/shard_map/ppermute | solution.py:344
  11.5 47.2 %collective-permute-start.1 = (bf16[384,4096]{1,0:T(8,128)(2,1)}, bf16[384,4096]{1,0:T(8,128)(2,1)}, u32[]{:S(2)}, u32[]{:S(2)}) collective-permute-start(bf16[384,4096]{1,0:T(8,128)(2,1)} %bitcast.20), channel_id=1, source_target_pairs={{0,1},{1,0},{2,3},{3,2},{4,5},{5,4},{6,7},{7,6},{8,9},{9,8},{10,11... | collective-permute-start | bytes 9437192 | tf_op jit(solution)/shard_map/ppermute | solution.py:344
  12.0 46.8 %collective-permute-start.2 = (bf16[384,4096]{1,0:T(8,128)(2,1)}, bf16[384,4096]{1,0:T(8,128)(2,1)}, u32[]{:S(2)}, u32[]{:S(2)}) collective-permute-start(bf16[384,4096]{1,0:T(8,128)(2,1)} %bitcast.22), channel_id=1, source_target_pairs={{0,1},{1,0},{2,3},{3,2},{4,5},{5,4},{6,7},{7,6},{8,9},{9,8},{10,11... | collective-permute-start | bytes 9437192 | tf_op jit(solution)/shard_map/ppermute | solution.py:344
  58.7 12.3 %copy-start = (bf16[16,8,8192]{2,1,0:T(8,128)(2,1)}, bf16[16,8,8192]{2,1,0:T(8,128)(2,1)S(1)}, u32[]{:S(2)}) copy-start(bf16[16,8,8192]{2,1,0:T(8,128)(2,1)S(1)} %all-to-all-done) | copy-start | bytes 6291460
  58.7 18.1 %copy-start.3 = (bf16[128,128]{1,0:T(8,128)(2,1)S(1)}, bf16[128,128]{1,0:T(8,128)(2,1)}, u32[]{:S(2)}) copy-start(bf16[128,128]{1,0:T(8,128)(2,1)} %get-tuple-element.12) | copy-start | bytes 98308
  58.7 47.2 %collective-permute-start.4 = (bf16[128,8192]{1,0:T(8,128)(2,1)S(1)}, bf16[128,8192]{1,0:T(8,128)(2,1)}, u32[]{:S(2)}, u32[]{:S(2)}) collective-permute-start(bf16[128,8192]{1,0:T(8,128)(2,1)S(1)} %bitcast.13), channel_id=1, source_target_pairs={{0,1},{1,0},{2,3},{3,2},{4,5},{5,4},{6,7},{7,6},{8,9},{9,8},{10,11... | collective-permute-start | bytes 6291464 | tf_op jit(solution)/shard_map/ppermute | solution.py:344
  71.0 31.3 %all-to-all-start.1 = ((bf16[16,8,4096]{2,1,0:T(8,128)(2,1)}), bf16[16,8,4096]{2,1,0:T(8,128)(2,1)S(1)}, u32[]{:S(2)}, u32[]{:S(2)}) async-start(bf16[16,8,4096]{2,1,0:T(8,128)(2,1)} %bitcast.25), calls=%async_computation.1 | async-start | bytes 2097152 | tf_op jit(solution)/shard_map/all_to_all | solution.py:340
  76.8 29.0 %collective-permute-start.3 = (bf16[1152,128]{1,0:T(8,128)(2,1)}, bf16[1152,128]{1,0:T(8,128)(2,1)S(1)}, u32[]{:S(2)}, u32[]{:S(2)}) collective-permute-start(bf16[1152,128]{1,0:T(8,128)(2,1)} %get-tuple-element.16), channel_id=1, source_target_pairs={{0,1},{1,0},{2,3},{3,2},{4,5},{5,4},{6,7},{7,6},{8,9},{9,8},{10,11... | collective-permute-start | bytes 884744 | tf_op jit(solution)/shard_map/ppermute | solution.py:344
  102.3 1.0 copy-start.1
  105.9 0.7 copy-start.2
where the time goes:
time: 117 us; the launch traced here: 116 us
  waiting for transfers between devices  71.4 us (61%)
  Pallas kernels  28.1 us (24%)
  starting transfers between devices  13.6 us (12%)
  local copies, waits for them, and re-layouts  2.38 us (2%)
    all_to_all x2, waiting for transfers between devices, exchange(): return lax.all_to_all(rows, 'ep', split_axis=0, concat_axis=0, tiled=True)  71.3 us
    all_to_all x2, starting transfers between devices, exchange(): return lax.all_to_all(rows, 'ep', split_axis=0, concat_axis=0, tiled=True)  13.1 us
    pallas_call x1, Pallas kernels, expert_terms(): pl.pallas_call(expert_kernel, in_specs=[vmem] + [anywhere] * 6, out_specs...  12.2 us
    pallas_call x1, Pallas kernels, weight_grads(): pl.pallas_call(weight_kernel, grid=(blocks,), in_specs=[pl.BlockSpec(coef...  9.6 us
    pallas_call x1, Pallas kernels, gather(): pl.pallas_call(functools.partial(gather_kernel, experts), in_specs=[anywh...  3.61 us
    pallas_call x1, Pallas kernels, combine(): pl.pallas_call(combine_kernel, in_specs=[anywhere] * 2, out_specs=anywher...  2.62 us
  transfers between devices with their start and end apart: 7, of which 2 were waited for; matrix products, arithmetic and copies ran while one was open for 1% of the time, Pallas kernels for 13%

commit v1 on v0

--- a/solution.py
+++ b/solution.py
@@ -10,8 +10,9 @@
 
 CAP = 8
 MIB = 1 << 20
-PIECES = 2
+PIECES = 1
 IN_FLIGHT = 3
+PASS = 192
 
 f32 = jnp.float32
 bf16 = jnp.bfloat16
@@ -97,7 +98,7 @@
 def gather(experts, ids, gates, tokens, grad_out):
     count, width = tokens.shape
     rows = experts * CAP
-    blocks = 8
+    blocks = 4
     block = 2 * width // blocks
     anywhere = pl.BlockSpec(memory_space=pl.ANY)
     return pl.pallas_call(
@@ -170,9 +171,14 @@
             load(n).wait()
             if n + IN_FLIGHT < len(units):
                 load(n + IN_FLIGHT).start()
-            first_s[k * hidden + at : k * hidden + at + size, :] = jnp.dot(
-                held(h, k, at, size)[...], turned_s[k // 2], preferred_element_type=f32
-            )
+            for m in range(0, size, PASS):
+                count = min(PASS, size - m)
+                to = k * hidden + at + m
+                first_s[to : to + count, :] = jnp.dot(
+                    held(h, k, at, size)[m : m + count, :],
+                    turned_s[k // 2],
+                    preferred_element_type=f32,
+                )
 
         step = 32
 
@@ -267,7 +273,7 @@
     whole = lambda i: (0, 0)
     x_at = pl.BlockSpec((rows, block), lambda i: (0, i))
     dy_at = pl.BlockSpec((rows, block), lambda i: (0, blocks + i))
-    rows_a, rows_b = in_hbm(rows_a), in_hbm(rows_b)
+    rows_b = in_hbm(rows_b)
     return pl.pallas_call(
         weight_kernel,
         grid=(blocks,),
@@ -280,29 +286,21 @@
             bytes_accessed=6 * hidden * width + 8 * rows * width,
             transcendentals=0,
         ),
-        compiler_params=pltpu.CompilerParams(vmem_limit_bytes=65472 * 1024),
+        compiler_params=pltpu.CompilerParams(vmem_limit_bytes=12 * MIB + 48 * rows * (hidden + block)),
     )(in_hbm(coef_a), in_hbm(coef_b), rows_a, rows_a, rows_b, rows_b)
 
 
-def combine_kernel(turned_ref, ret_ref, out_ref, turned_s, ret_s, out_s, sems, out_sems):
-    blocks, _, block = ret_s.shape
-
-    def load(i):
-        cols = pl.ds(i * block, block)
-        return pltpu.make_async_copy(ret_ref.at[:, cols], ret_s.at[i], sems.at[i])
+def combine_kernel(turned_ref, ret_ref, out_ref, out_s, out_sems):
+    blocks, _, block = out_s.shape
 
     def store(i):
         cols = pl.ds(i * block, block)
         return pltpu.make_async_copy(out_s.at[i], out_ref.at[:, cols], out_sems.at[i])
 
-    first = pltpu.make_async_copy(turned_ref, turned_s, sems.at[blocks])
-    first.start()
-    for i in range(blocks):
-        load(i).start()
-    first.wait()
-    for i in range(blocks):
-        load(i).wait()
-        out_s[i] = jnp.dot(turned_s[...], ret_s[i], preferred_element_type=f32).astype(bf16)
+    for i in range(blocks):
+        out_s[i] = jnp.dot(
+            turned_ref[...], ret_ref[:, i * block : (i + 1) * block], preferred_element_type=f32
+        ).astype(bf16)
         store(i).start()
     for i in range(blocks):
         store(i).wait()
@@ -311,19 +309,15 @@
 def combine(turned, ret):
     count, rows = turned.shape
     width = ret.shape[1]
-    blocks = 4
-    block = width // blocks
-    anywhere = pl.BlockSpec(memory_space=pl.ANY)
+    blocks = 2
+    vmem = pl.BlockSpec(memory_space=pltpu.VMEM)
     return pl.pallas_call(
         combine_kernel,
-        in_specs=[anywhere] * 2,
-        out_specs=anywhere,
+        in_specs=[vmem] * 2,
+        out_specs=pl.BlockSpec(memory_space=pl.ANY),
         out_shape=pltpu.HBM((count, width), bf16),
         scratch_shapes=[
-            pltpu.VMEM((count, rows), bf16),
-            pltpu.VMEM((blocks, rows, block), bf16),
-            pltpu.VMEM((blocks, count, block), bf16),
-            pltpu.SemaphoreType.DMA((blocks + 1,)),
+            pltpu.VMEM((blocks, count, width // blocks), bf16),
             pltpu.SemaphoreType.DMA((blocks,)),
         ],
         name="combine",
@@ -333,7 +327,7 @@
         compiler_params=pltpu.CompilerParams(
             vmem_limit_bytes=8 * MIB + 4 * (rows + count) * width
         ),
-    )(in_hbm(turned), in_hbm(ret))
+    )(in_vmem(turned), in_vmem(ret))
 
 
 def exchange(rows):

time: 117 us -> 112 us (0.957)
  Pallas kernels: 28.1 us -> 23.5 us
  local copies, waits for them, and re-layouts: 2.38 us -> 0.81 us
  waiting for transfers between devices: 71.4 us -> 72.7 us
    pallas_call x1, Pallas kernels: 9.6 us -> 8.14 us  [weight_grads(): pl.pallas_call(weight_kernel, grid=(blocks,), in_specs=[pl.BlockSpec(coef...]
    all_to_all x2, waiting for transfers between devices: 71.3 us -> 72.7 us  [exchange(): return lax.all_to_all(rows, 'ep', split_axis=0, concat_axis=0, tiled=True)]
    pallas_call x1, Pallas kernels: 2.62 us -> 1.27 us  [combine(): pl.pallas_call(combine_kernel, in_specs=[vmem] * 2, out_specs=pl.BlockSpe...]
    pallas_call x1, Pallas kernels: 12.2 us -> 11 us  [expert_terms(): pl.pallas_call(expert_kernel, in_specs=[vmem] + [anywhere] * 6, out_specs...]
  transfers between devices with their start and end apart: 7 -> 7, of which waited for: 2 -> 2; matrix products, arithmetic and copies ran while one was open for 1% -> 0% of each run, Pallas kernels for 13% -> 11%
where the time goes in v1:
time: 112 us; the launch traced here: 111 us
  waiting for transfers between devices  72.7 us (65%)
  Pallas kernels  23.5 us (21%)
  starting transfers between devices  13.6 us (12%)
    all_to_all x2, waiting for transfers between devices, exchange(): return lax.all_to_all(rows, 'ep', split_axis=0, concat_axis=0, tiled=True)  72.7 us
    all_to_all x2, starting transfers between devices, exchange(): return lax.all_to_all(rows, 'ep', split_axis=0, concat_axis=0, tiled=True)  13.1 us
    pallas_call x1, Pallas kernels, expert_terms(): pl.pallas_call(expert_kernel, in_specs=[vmem] + [anywhere] * 6, out_specs...  11 us
    pallas_call x1, Pallas kernels, weight_grads(): pl.pallas_call(weight_kernel, grid=(blocks,), in_specs=[pl.BlockSpec(coef...  8.14 us
    pallas_call x1, Pallas kernels, gather(): pl.pallas_call(functools.partial(gather_kernel, experts), in_specs=[anywh...  3.12 us
  transfers between devices with their start and end apart: 7, of which 2 were waited for; matrix products, arithmetic and copies ran while one was open for 0% of the time, Pallas kernels for 11%

profile of v1, /device:TPU:8, one launch (start us, length us, event | category | flops | bytes accessed | tf_op | source)
XLA Modules:
  0.0 111.4 jit_solution(5450617998344144330)
XLA Ops:
  0.6 3.1 %gather.1 = (bf16[128,8192]{1,0:T(8,128)(2,1)}, bf16[128,128]{1,0:T(8,128)(2,1)}) custom-call(s32[8,128]{1,0:T(8,128)} %bitcast.27, f32[8,128]{1,0:T(8,128)} %bitcast.28, bf16[128,4096]{1,0:T(8,128)(2,1)} %tok_ref.1, bf16[128,4096]{1,0:T(8,128)(2,1)} %dy_ref.1), custom_call_target="tpu_custom_call" | custom-call | flops 268435456 | bytes 4194304 | tf_op jit(solution)/shard_map/gather/pallas_call | solution.py:104
  3.8 7.2 %all-to-all-start = ((bf16[16,8,8192]{2,1,0:T(8,128)(2,1)}), bf16[16,8,8192]{2,1,0:T(8,128)(2,1)S(1)}, u32[]{:S(2)}, u32[]{:S(2)}) async-start(bf16[16,8,8192]{2,1,0:T(8,128)(2,1)} %bitcast.25), calls=%async_computation | async-start | bytes 4194304 | tf_op jit(solution)/shard_map/all_to_all | solution.py:334
  11.0 0.0 collective-permute-start
  11.0 0.5 collective-permute-start.1
  11.5 0.1 collective-permute-start.2
  11.6 46.6 %all-to-all-done = bf16[16,8,8192]{2,1,0:T(8,128)(2,1)S(1)} async-done(((bf16[16,8,8192]{2,1,0:T(8,128)(2,1)}), bf16[16,8,8192]{2,1,0:T(8,128)(2,1)S(1)}, u32[]{:S(2)}, u32[]{:S(2)}) %all-to-all-start) | async-done | bytes 2097184 | tf_op jit(solution)/shard_map/all_to_all | solution.py:334
  58.2 0.0 copy-start.1
  58.2 0.0 collective-permute-start.4
  58.2 0.0 collective-permute-done.gate_b
  58.2 0.0 collective-permute-done.1.up_b
  58.2 0.0 collective-permute-done.2.down_b
  58.3 11.0 %expert_terms.1 = (bf16[128,4096]{1,0:T(8,128)(2,1)}, bf16[1152,128]{1,0:T(8,128)(2,1)}, bf16[1152,128]{1,0:T(8,128)(2,1)}) custom-call(bf16[128,8192]{1,0:T(8,128)(2,1)S(1)} %bitcast.14, bf16[384,4096]{1,0:T(8,128)(2,1)} %bitcast.20, bf16[384,4096]{1,0:T(8,128)(2,1)} %bitcast.22, bf16[384,4096]{1,0:T(8,128)(2,1)} %bitcast.24, ...), custom_call_target="tpu_custom_call" | custom-call | flops 4026531840 | bytes 22020096 | tf_op jit(solution)/shard_map/expert_terms/pallas_call | solution.py:226
  69.2 5.8 %all-to-all-start.1 = ((bf16[16,8,4096]{2,1,0:T(8,128)(2,1)}), bf16[16,8,4096]{2,1,0:T(8,128)(2,1)S(1)}, u32[]{:S(2)}, u32[]{:S(2)}) async-start(bf16[16,8,4096]{2,1,0:T(8,128)(2,1)} %bitcast.26), calls=%async_computation.1 | async-start | bytes 2097152 | tf_op jit(solution)/shard_map/all_to_all | solution.py:334
  75.1 0.0 collective-permute-start.3
  75.1 0.0 copy-done.1
  75.1 0.1 copy.11
  75.2 26.1 %all-to-all-done.1 = bf16[16,8,4096]{2,1,0:T(8,128)(2,1)S(1)} async-done(((bf16[16,8,4096]{2,1,0:T(8,128)(2,1)}), bf16[16,8,4096]{2,1,0:T(8,128)(2,1)S(1)}, u32[]{:S(2)}, u32[]{:S(2)}) %all-to-all-start.1) | async-done | bytes 1048608 | tf_op jit(solution)/shard_map/all_to_all | solution.py:334
  101.3 1.3 %combine.1 = bf16[128,4096]{1,0:T(8,128)(2,1)} custom-call(bf16[128,128]{1,0:T(8,128)(2,1)S(1)} %bitcast.18, bf16[128,4096]{1,0:T(8,128)(2,1)S(1)} %bitcast.17), custom_call_target="tpu_custom_call" | custom-call | flops 134217728 | bytes 2097152 | tf_op jit(solution)/shard_map/combine/pallas_call | solution.py:314
  102.6 0.0 collective-permute-done.3.coef_b
  102.6 0.0 copy-start
  102.6 0.0 collective-permute-done.4.x_b.dy_b
  102.6 0.7 copy-done
  103.3 8.1 %weight_grads.1 = (bf16[384,4096]{1,0:T(8,128)(2,1)}, bf16[384,4096]{1,0:T(8,128)(2,1)}, bf16[384,4096]{1,0:T(8,128)(2,1)}) custom-call(bf16[1152,128]{1,0:T(8,128)(2,1)} %get-tuple-element.15.coef_a, bf16[1152,128]{1,0:T(8,128)(2,1)} %copy-done, bf16[128,8192]{1,0:T(8,128)(2,1)S(1)} %bitcast.15, bf16[128,8192]{1,0:T(8,128)(2,1)S(1)} %bitcast.16, ...), custom_call_target="tpu_custom_call" | custom-call | flops 2415919104 | bytes 13631488 | tf_op jit(solution)/shard_map/weight_grads/pallas_call | solution.py:277
Async XLA Ops:
  3.8 54.5 %all-to-all-start = ((bf16[16,8,8192]{2,1,0:T(8,128)(2,1)}), bf16[16,8,8192]{2,1,0:T(8,128)(2,1)S(1)}, u32[]{:S(2)}, u32[]{:S(2)}) async-start(bf16[16,8,8192]{2,1,0:T(8,128)(2,1)} %bitcast.25), calls=%async_computation | async-start | bytes 4194304 | tf_op jit(solution)/shard_map/all_to_all | solution.py:334
  11.0 47.2 %collective-permute-start = (bf16[384,4096]{1,0:T(8,128)(2,1)}, bf16[384,4096]{1,0:T(8,128)(2,1)}, u32[]{:S(2)}, u32[]{:S(2)}) collective-permute-start(bf16[384,4096]{1,0:T(8,128)(2,1)} %bitcast.19), channel_id=1, source_target_pairs={{0,1},{1,0},{2,3},{3,2},{4,5},{5,4},{6,7},{7,6},{8,9},{9,8},{10,11... | collective-permute-start | bytes 9437192 | tf_op jit(solution)/shard_map/ppermute | solution.py:338
  11.0 47.2 %collective-permute-start.1 = (bf16[384,4096]{1,0:T(8,128)(2,1)}, bf16[384,4096]{1,0:T(8,128)(2,1)}, u32[]{:S(2)}, u32[]{:S(2)}) collective-permute-start(bf16[384,4096]{1,0:T(8,128)(2,1)} %bitcast.21), channel_id=1, source_target_pairs={{0,1},{1,0},{2,3},{3,2},{4,5},{5,4},{6,7},{7,6},{8,9},{9,8},{10,11... | collective-permute-start | bytes 9437192 | tf_op jit(solution)/shard_map/ppermute | solution.py:338
  11.5 46.7 %collective-permute-start.2 = (bf16[384,4096]{1,0:T(8,128)(2,1)}, bf16[384,4096]{1,0:T(8,128)(2,1)}, u32[]{:S(2)}, u32[]{:S(2)}) collective-permute-start(bf16[384,4096]{1,0:T(8,128)(2,1)} %bitcast.23), channel_id=1, source_target_pairs={{0,1},{1,0},{2,3},{3,2},{4,5},{5,4},{6,7},{7,6},{8,9},{9,8},{10,11... | collective-permute-start | bytes 9437192 | tf_op jit(solution)/shard_map/ppermute | solution.py:338
  58.2 16.9 %copy-start.1 = (bf16[128,128]{1,0:T(8,128)(2,1)S(1)}, bf16[128,128]{1,0:T(8,128)(2,1)}, u32[]{:S(2)}) copy-start(bf16[128,128]{1,0:T(8,128)(2,1)} %get-tuple-element.12) | copy-start | bytes 98308
  58.2 44.4 %collective-permute-start.4 = (bf16[128,8192]{1,0:T(8,128)(2,1)S(1)}, bf16[128,8192]{1,0:T(8,128)(2,1)}, u32[]{:S(2)}, u32[]{:S(2)}) collective-permute-start(bf16[128,8192]{1,0:T(8,128)(2,1)S(1)} %bitcast.13), channel_id=1, source_target_pairs={{0,1},{1,0},{2,3},{3,2},{4,5},{5,4},{6,7},{7,6},{8,9},{9,8},{10,11... | collective-permute-start | bytes 6291464 | tf_op jit(solution)/shard_map/ppermute | solution.py:338
  69.2 32.1 %all-to-all-start.1 = ((bf16[16,8,4096]{2,1,0:T(8,128)(2,1)}), bf16[16,8,4096]{2,1,0:T(8,128)(2,1)S(1)}, u32[]{:S(2)}, u32[]{:S(2)}) async-start(bf16[16,8,4096]{2,1,0:T(8,128)(2,1)} %bitcast.26), calls=%async_computation.1 | async-start | bytes 2097152 | tf_op jit(solution)/shard_map/all_to_all | solution.py:334
  75.1 27.5 %collective-permute-start.3 = (bf16[1152,128]{1,0:T(8,128)(2,1)}, bf16[1152,128]{1,0:T(8,128)(2,1)S(1)}, u32[]{:S(2)}, u32[]{:S(2)}) collective-permute-start(bf16[1152,128]{1,0:T(8,128)(2,1)} %get-tuple-element.16), channel_id=1, source_target_pairs={{0,1},{1,0},{2,3},{3,2},{4,5},{5,4},{6,7},{7,6},{8,9},{9,8},{10,11... | collective-permute-start | bytes 884744 | tf_op jit(solution)/shard_map/ppermute | solution.py:338
  102.6 0.7 copy-start
